TPU v7x, 512 devices: a whole 4x8x8 slice. The times are simulated.
512 devices in a mesh: blk: 256 (over z, x_hi, y, core), seg: 2 (over x_lo).
Axes of the slice: x: 4 (x_hi: 2, x_lo: 2; x = x_hi * 2 + x_lo), y: 8, z: 8, core: 2. Of those that a mesh axis runs over, the one named last changes fastest.
Arguments:
- traces: float32 [4096, 16, 1024], P('blk', 'seg'), may hold values from -1140 to 1140
- mask: int32 [4096, 4, 16], P('blk'), may hold values from 0 to 1, as said below
- plan: int32 [256, 4], P('blk'), may hold values from 0 to 3, each once within a row
Outputs:
- correlations: bfloat16 [4, 4096, 16, 512], P('seg', 'blk')
Inputs may be any that keep to these rules, and one draw needn't show every extreme that they name: A channel is never paired with itself: mask[a 16 + i, 0, i] is 0. Each row of plan names every distance 0 to 3 once.
All inputs are finite; a program needn't handle non-finite values.
Results may differ from a plain program's by a relative error of at most 0.011.
Values may be sent and summed in bfloat16 or wider, within the bound.
No kernel may reach another device: no remote copies, remote signals or barrier semaphores. Data moves between devices by JAX's collectives and lax.ppermute only.
A program may use at most 64 MiB of HBM per device.

v0:
```python
import functools
import math

import jax
import jax.numpy as jnp
import ml_dtypes
import numpy as np
from jax import lax
from jax.experimental import pallas as pl
from jax.experimental.pallas import tpu as pltpu
from jax.sharding import PartitionSpec as P

EPS = 1e-05
STEPS = 4
F32 = jnp.float32
BF16 = jnp.bfloat16
VMEM = pl.BlockSpec(memory_space=pltpu.VMEM)
SMEM = pl.BlockSpec(memory_space=pltpu.SMEM)
HBM = pl.BlockSpec(memory_space=pltpu.HBM)
WIDTH = 256
REACH = 128


def angle_table(rows, cols, length):
    product = np.arange(rows)[:, None] * np.arange(cols)[None, :] % (2 * length)
    return product.astype(np.float32) * np.float32(math.pi / length)


def wave_table(length):
    angles = angle_table(length // 2, length, length)
    return np.stack((np.cos(angles), np.sin(angles))).astype(ml_dtypes.bfloat16)


def fill_box(box_ref, half):
    left = lax.broadcasted_iota(jnp.int32, box_ref.shape, 0) - REACH
    right = lax.broadcasted_iota(jnp.int32, box_ref.shape, 1)
    box_ref[...] = jnp.where(jnp.abs(left - right) <= half, 1.0, 0.0).astype(BF16)


def box_sum(values, box, col):
    low = max(0, col - REACH)
    high = min(values.shape[1], col + WIDTH + REACH)
    tile = box[low - col + REACH : high - col + REACH, :]
    return jnp.dot(values[:, low:high], tile, preferred_element_type=F32)


def normalize_kernel(half, traces_hbm, out_ref, traces_ref, mag_ref, box_ref, sems):
    copies = []
    for q, col in enumerate(range(0, traces_ref.shape[1], WIDTH)):
        cols = slice(col, col + WIDTH)
        copies.append(pltpu.make_async_copy(traces_hbm.at[:, cols], traces_ref.at[:, cols], sems.at[q]))
        copies[-1].start()
    fill_box(box_ref, half)
    for q in range(len(copies) + 1):
        if q < len(copies):
            copies[q].wait()
            cols = slice(q * WIDTH, (q + 1) * WIDTH)
            mag_ref[:, cols] = jnp.abs(traces_ref[:, cols]).astype(BF16)
        if q > 0:
            cols = slice((q - 1) * WIDTH, q * WIDTH)
            level = box_sum(mag_ref, box_ref, (q - 1) * WIDTH) / (2 * half + 1)
            out_ref[:, cols] = (traces_ref[:, cols] / (level + EPS)).astype(BF16)


def start_tables(wave_hbm, wave_ref, sems):
    copies = []
    for q, col in enumerate(range(0, wave_ref.shape[2], WIDTH)):
        cols = slice(col, col + WIDTH)
        copies.append(pltpu.make_async_copy(wave_hbm.at[:, :, cols], wave_ref.at[:, :, cols], sems.at[q]))
        copies[-1].start()
    return copies


def whiten_into(x_ref, wave_ref, box_ref, amp_ref, work_ref, tile_ref, out_ref, half, copies=()):
    rows, length = x_ref.shape
    mid = length // 2
    runs = length // 128
    both = jnp.concatenate([x_ref[:, :mid], x_ref[:, mid:]], axis=0)
    lane = lax.broadcasted_iota(jnp.int32, (1, WIDTH), 1)
    even = (lane & 1) == 0
    sign = (1 - (lane & 2)).astype(F32)
    for q, col in enumerate(range(0, length, WIDTH)):
        cols = slice(col, col + WIDTH)
        if copies:
            copies[q].wait()
        cos_part = jnp.dot(both, wave_ref[0, :, cols], preferred_element_type=F32)
        sin_part = jnp.dot(both, wave_ref[1, :, cols], preferred_element_type=F32)
        re = cos_part[:rows] + sign * jnp.where(even, cos_part[rows:], -sin_part[rows:])
        im = sin_part[:rows] + sign * jnp.where(even, sin_part[rows:], cos_part[rows:])
        work_ref[0, :, cols] = re
        work_ref[1, :, cols] = im
        amp_ref[:, cols] = jnp.sqrt(re * re + im * im).astype(BF16)
    for col in range(0, length, WIDTH):
        smooth = box_sum(amp_ref, box_ref, col) / (2 * half + 1)
        scale = 1.0 / (smooth + EPS)
        for c in range(2):
            for lane in range(0, WIDTH, 128):
                run = (col + lane) // 128
                white = work_ref[c, :, col + lane : col + lane + 128] * scale[:, lane : lane + 128]
                tile_ref[pl.ds(c * runs + run, rows, stride=2 * runs), :] = white
    out_ref[...] = tile_ref[...].astype(BF16).reshape(out_ref.shape)


def whiten_kernel(half, x_ref, wave_hbm, out_ref, wave_ref, box_ref, amp_ref, work_ref, tile_ref, sems):
    copies = start_tables(wave_hbm, wave_ref, sems)
    fill_box(box_ref, half)
    whiten_into(x_ref, wave_ref, box_ref, amp_ref, work_ref, tile_ref, out_ref, half, copies)


def cross_into(mine_ref, far_ref, pair_ref, cross_ref):
    chans, wins, height, _ = mine_ref.shape
    runs = height // 2
    group = 8
    parts = chans // group

    def step(at, carry):
        i = at // parts
        part = at % parts
        mine = [mine_ref[i, w] for w in range(wins)]
        for j in range(group):
            terms = [mine[w] * far_ref[part * group + j, w] for w in range(wins)]
            while len(terms) > wins // 4:
                terms = [terms[k] + terms[k + 1] for k in range(0, len(terms), 2)]
            wide = [term.astype(F32) for term in terms]
            total = sum(wide[1:], wide[0])
            pair_ref[at, pl.ds(j, runs, stride=group), :] = total[:runs] + total[runs:]
        return carry

    lax.fori_loop(0, chans * parts, step, 0, unroll=2)
    for run in range(runs):
        tile = pair_ref[:, run * group : (run + 1) * group, :].reshape(chans * chans, 128)
        cross_ref[:, run * 128 : (run + 1) * 128] = tile.astype(BF16)


def flip_of(distance, per_row):
    blk = lax.axis_index("blk")
    chip = blk // 2
    core = blk % 2
    wrap = (chip % per_row == per_row - 1).astype(jnp.int32)
    ahead = ((chip + 1) % per_row == per_row - 1).astype(jnp.int32)
    one = jnp.where(core == 0, 0, wrap)
    three = jnp.where(core == 0, wrap, jnp.bitwise_xor(wrap, ahead))
    return jnp.where(distance == 1, one, jnp.where(distance == 2, wrap, jnp.where(distance == 3, three, 0)))


def half_kernel(half, per_row, second, scale, plan_ref, own_ref, other_ref, y13_ref, y2_ref, wave_hbm, *refs):
    if second:
        part_ref, mask_ref, out_ref = refs[:3]
        refs = refs[3:]
    else:
        out_ref = refs[0]
        refs = refs[1:]
    wave_ref, box_ref, amp_ref, x_ref, work_ref, tile_ref, mine_ref, far_ref, pair_ref, cross_ref, sems = refs
    copies = start_tables(wave_hbm, wave_ref, sems)
    fill_box(box_ref, half)
    seg = lax.axis_index("seg")

    for n in range(out_ref.shape[0]):
        distance = plan_ref[0, seg * out_ref.shape[0] + n]
        which = jnp.bitwise_xor(flip_of(distance, per_row), second)

        def copy(when, source, target):
            @pl.when(when)
            def _():
                target[...] = source[...]

        for h, ref in enumerate((own_ref, other_ref)):
            copy(which == h, ref, mine_ref)
            copy((which == h) & (distance == 0), ref, far_ref)
        for d, y_ref in ((1, y13_ref.at[0]), (2, y2_ref), (3, y13_ref.at[1])):
            copy(distance == d, y_ref, x_ref)
        if n == 0:
            for table in copies:
                table.wait()

        @pl.when(distance > 0)
        def _():
            whiten_into(x_ref, wave_ref, box_ref, amp_ref, work_ref, tile_ref, far_ref, half)

        cross_into(mine_ref, far_ref, pair_ref, cross_ref)
        folded = lax.dot_general(
            cross_ref[...], wave_ref[0], (((1,), (1,)), ((), ())), preferred_element_type=F32
        )
        once = cross_ref[:, 0:1].astype(F32)
        if second:
            keep = mask_ref[distance]
            for col in range(0, folded.shape[1], 128):
                cols = slice(col, col + 128)
                part = (2.0 * folded[:, cols] - once) * scale
                part = (part + part_ref[n, :, cols]) * keep
                out_ref[n, :, cols] = part.astype(BF16)
        else:
            out_ref[n] = (2.0 * folded - once) * scale


def per_device(per_row, traces, mask, plan):
    chans, wins, length = traces.shape
    half = length // 16
    lags = length // 2
    rows = chans * wins
    blocks = lax.axis_size("blk")
    segs = lax.axis_size("seg")
    steps = STEPS // segs
    core = lax.axis_index("blk") % 2

    def send(array, source):
        pairs = []
        for b in range(blocks):
            for s in range(segs):
                where = source(b, s)
                if where is not None and where[0] < blocks:
                    pairs.append((where[0] * segs + where[1], b * segs + s))
        return lax.ppermute(array, ("blk", "seg"), pairs)

    def ahead(b, s, by):
        chip = b // 2
        wraps = (chip % per_row == per_row - 1) and (b + by) // 2 > chip
        return (b + by, 1 - s if wraps else s)

    def in_hbm(array):
        return pltpu.with_memory_space_constraint(array, pltpu.HBM)

    wave_tab = in_hbm(jnp.asarray(wave_table(length)))
    runs = length // 128
    white_shape = (chans, wins, 2 * runs, 128)
    scale = 1.0 / math.sqrt(wins * segs * length)
    quarters = length // WIDTH
    box = pltpu.VMEM((WIDTH + 2 * REACH, WIDTH), BF16)
    wave = pltpu.VMEM(wave_tab.shape, BF16)
    amp = pltpu.VMEM((rows, length), BF16)
    work = pltpu.VMEM((2, rows, length), F32)
    tile = pltpu.VMEM((rows * 2 * runs, 128), F32)
    white = pltpu.VMEM(white_shape, BF16)

    x = pl.pallas_call(
        functools.partial(normalize_kernel, half),
        out_shape=jax.ShapeDtypeStruct((rows, length), BF16),
        in_specs=[HBM],
        out_specs=VMEM,
        scratch_shapes=[
            pltpu.VMEM((rows, length), F32),
            amp,
            box,
            pltpu.SemaphoreType.DMA((quarters,)),
        ],
        compiler_params=pltpu.CompilerParams(vmem_limit_bytes=6 << 20),
        name="normalize",
    )(in_hbm(traces.reshape(rows, length)))

    def whiten(array):
        return pl.pallas_call(
            functools.partial(whiten_kernel, half),
            out_shape=jax.ShapeDtypeStruct(white_shape, BF16),
            in_specs=[VMEM, HBM],
            out_specs=VMEM,
            scratch_shapes=[wave, box, amp, work, tile, pltpu.SemaphoreType.DMA((quarters,))],
            compiler_params=pltpu.CompilerParams(vmem_limit_bytes=12 << 20),
            name="whiten",
        )(array, wave_tab)

    def half_sums(second, dtype, *args):
        return pl.pallas_call(
            functools.partial(half_kernel, half, per_row, second, scale),
            out_shape=jax.ShapeDtypeStruct((steps, chans * chans, lags), dtype),
            in_specs=[SMEM] + [VMEM] * 4 + [HBM] + [VMEM] * (2 * second),
            out_specs=VMEM,
            scratch_shapes=[
                wave,
                box,
                amp,
                amp,
                work,
                tile,
                white,
                white,
                pltpu.VMEM((chans * chans // 8, 8 * runs, 128), F32),
                pltpu.VMEM((chans * chans, length), BF16),
                pltpu.SemaphoreType.DMA((quarters,)),
            ],
            compiler_params=pltpu.CompilerParams(vmem_limit_bytes=24 << 20),
            name="second" if second else "first",
        )(plan, own, other, *args)

    keep = jnp.transpose(mask, (1, 0, 2)).reshape(STEPS, chans * chans, 1)
    keep = jnp.broadcast_to(keep, (STEPS, chans * chans, 128)).astype(F32)

    def next_block(b, s):
        return ahead(b, s, 1) if b % 2 else (b + 1, s)

    y2 = send(x, lambda b, s: ahead(b, s, 2))
    o = send(x, lambda b, s: (b, 1 - s))
    own = whiten(x)
    y2, own = lax.optimization_barrier((y2, own))
    y2o = send(y2, lambda b, s: (b, 1 - s))
    y13 = send(jnp.stack((x, y2)), next_block)
    other = whiten(o)
    y2o, other = lax.optimization_barrier((y2o, other))
    y13o = send(jnp.stack((o, y2o)), next_block)
    part = half_sums(0, F32, y13, y2, wave_tab)
    out = half_sums(1, BF16, y13o, y2o, wave_tab, part, keep)
    return out.reshape(steps, chans, chans, lags)


def solution(mesh):
    return jax.shard_map(
        functools.partial(per_device, 8),
        mesh=mesh,
        in_specs=(P("blk", "seg", None), P("blk", None, None), P("blk", None)),
        out_specs=P("seg", "blk", None, None),
        check_vma=False,
    )
```

profile of v0, /device:TPU:255, one launch (start us, length us, event | category | flops | bytes accessed | tf_op | source)
XLA Modules:
  0.0 52.2 jit_solution(800222220087496598)
XLA Ops:
  0.0 1.7 %normalize.1.x_ref = bf16[128,1024]{1,0:T(8,128)(2,1)S(1)} custom-call(f32[128,1024]{1,0:T(8,128)} %bitcast.12), custom_call_target="tpu_custom_call" | custom-call | tf_op jit(solution)/shard_map/normalize/pallas_call | solution.py:235
  1.7 3.0 %collective-permute-start = (bf16[128,1024]{1,0:T(8,128)(2,1)S(1)}, bf16[128,1024]{1,0:T(8,128)(2,1)S(1)}, u32[]{:S(2)}, u32[]{:S(2)}) collective-permute-start(bf16[128,1024]{1,0:T(8,128)(2,1)S(1)} %normalize.1.x_ref), channel_id=1, source_target_pairs={{4,0},{5,1},{6,2},{7,3},{8,4},{9,5},{10,6},{11,7},{12,8},{13,9},{1... | collective-permute-start | bytes 786440 | tf_op jit(solution)/shard_map/ppermute | solution.py:213
  4.7 2.5 %collective-permute-start.2 = (bf16[128,1024]{1,0:T(8,128)(2,1)S(1)}, bf16[128,1024]{1,0:T(8,128)(2,1)S(1)}, u32[]{:S(2)}, u32[]{:S(2)}) collective-permute-start(bf16[128,1024]{1,0:T(8,128)(2,1)S(1)} %normalize.1.x_ref), channel_id=1, source_target_pairs={{1,0},{0,1},{3,2},{2,3},{5,4},{4,5},{7,6},{6,7},{9,8},{8,9},{11,10... | collective-permute-start | bytes 786440 | tf_op jit(solution)/shard_map/ppermute | solution.py:213
  7.1 2.9 %whiten.2.own_ref = bf16[16,8,16,128]{3,2,1,0:T(8,128)(2,1)S(1)} custom-call(bf16[128,1024]{1,0:T(8,128)(2,1)S(1)} %normalize.1.x_ref, bf16[2,512,1024]{2,1,0:T(8,128)(2,1)} %constant.2.clone.wave_hbm), custom_call_target="tpu_custom_call" | custom-call | tf_op jit(solution)/shard_map/whiten/pallas_call | solution.py:251
  10.1 6.1 %collective-permute-done.y2_ref = bf16[128,1024]{1,0:T(8,128)(2,1)S(1)} collective-permute-done((bf16[128,1024]{1,0:T(8,128)(2,1)S(1)}, bf16[128,1024]{1,0:T(8,128)(2,1)S(1)}, u32[]{:S(2)}, u32[]{:S(2)}) %collective-permute-start) | collective-permute-done | bytes 262176 | tf_op jit(solution)/shard_map/ppermute | solution.py:213
  16.2 1.9 %collective-permute-start.1 = (bf16[128,1024]{1,0:T(8,128)(2,1)S(1)}, bf16[128,1024]{1,0:T(8,128)(2,1)S(1)}, u32[]{:S(2)}, u32[]{:S(2)}) collective-permute-start(bf16[128,1024]{1,0:T(8,128)(2,1)S(1)} %collective-permute-done.y2_ref), channel_id=1, source_target_pairs={{1,0},{0,1},{3,2},{2,3},{5,4},{4,5},{7,6},{6,7},{9,8},{8,9},{11,10... | collective-permute-start | bytes 786440 | tf_op jit(solution)/shard_map/ppermute | solution.py:213
  18.1 0.1 pad_maximum_fusion.1
  18.2 0.0 copy-start.1
  18.2 0.0 copy-start
  18.2 3.4 %collective-permute-start.4 = (bf16[2,128,1024]{2,1,0:T(8,128)(2,1)S(1)}, bf16[2,128,1024]{2,1,0:T(8,128)(2,1)S(1)}, u32[]{:S(2)}, u32[]{:S(2)}) collective-permute-start(bf16[2,128,1024]{2,1,0:T(8,128)(2,1)S(1)} %pad_maximum_fusion.1), channel_id=1, source_target_pairs={{2,0},{3,1},{4,2},{5,3},{6,4},{7,5},{8,6},{9,7},{10,8},{11,9},{12,... | collective-permute-start | bytes 1572872 | tf_op jit(solution)/shard_map/ppermute | solution.py:213
  21.7 0.0 collective-permute-done.2.x_ref
  21.7 2.9 %whiten.3.other_ref = bf16[16,8,16,128]{3,2,1,0:T(8,128)(2,1)S(1)} custom-call(bf16[128,1024]{1,0:T(8,128)(2,1)S(1)} %collective-permute-done.2.x_ref, bf16[2,512,1024]{2,1,0:T(8,128)(2,1)} %constant.2.clone.wave_hbm), custom_call_target="tpu_custom_call" | custom-call | tf_op jit(solution)/shard_map/whiten/pallas_call | solution.py:251
  24.6 0.0 collective-permute-done.1.y2_ref
  24.6 0.8 %pad_maximum_fusion = bf16[2,128,1024]{2,1,0:T(8,128)(2,1)} fusion(bf16[1,128,1024]{2,1,0:T(8,128)(2,1)S(1)} %bitcast.10, bf16[1,128,1024]{2,1,0:T(8,128)(2,1)S(1)} %bitcast.11), kind=kLoop, calls=%fused_computation | loop fusion | flops 262144 | bytes 1048576 | tf_op jit(solution)/shard_map/stack | solution.py:298
  25.4 4.1 %collective-permute-start.3 = (bf16[2,128,1024]{2,1,0:T(8,128)(2,1)}, bf16[2,128,1024]{2,1,0:T(8,128)(2,1)S(1)}, u32[]{:S(2)}, u32[]{:S(2)}) collective-permute-start(bf16[2,128,1024]{2,1,0:T(8,128)(2,1)} %pad_maximum_fusion), channel_id=1, source_target_pairs={{2,0},{3,1},{4,2},{5,3},{6,4},{7,5},{8,6},{9,7},{10,8},{11,9},{12,... | collective-permute-start | bytes 1572872 | tf_op jit(solution)/shard_map/ppermute | solution.py:213
  29.6 0.0 copy-done.1
  29.6 0.1 convert_element_type.9
  29.7 4.5 %collective-permute-done.4.y13_ref = bf16[2,128,1024]{2,1,0:T(8,128)(2,1)S(1)} collective-permute-done((bf16[2,128,1024]{2,1,0:T(8,128)(2,1)S(1)}, bf16[2,128,1024]{2,1,0:T(8,128)(2,1)S(1)}, u32[]{:S(2)}, u32[]{:S(2)}) %collective-permute-start.4) | collective-permute-done | bytes 524320 | tf_op jit(solution)/shard_map/ppermute | solution.py:213
  34.1 0.0 copy-done
  34.1 8.5 %first.1.refs_0_ = f32[2,256,512]{2,1,0:T(8,128)S(1)} custom-call(s32[1,4]{1,0:T(1,128)S(1)} %copy-done, bf16[16,8,16,128]{3,2,1,0:T(8,128)(2,1)S(1)} %whiten.2.own_ref, bf16[16,8,16,128]{3,2,1,0:T(8,128)(2,1)S(1)} %whiten.3.other_ref, bf16[2,128,1024]{2,1,0:T(8,128)(2,1)S(1)} %collective-permute-done.4.y13_ref, ...), custom_call_target="tpu_custom_call" | custom-call | tf_op jit(solution)/shard_map/first/pallas_call | solution.py:262
  42.7 0.0 collective-permute-done.3.y13_ref
  42.7 0.2 broadcast_in_dim.2.refs_1_
  42.9 9.4 %second.1 = bf16[2,256,512]{2,1,0:T(8,128)(2,1)} custom-call(s32[1,4]{1,0:T(1,128)S(1)} %copy-done, bf16[16,8,16,128]{3,2,1,0:T(8,128)(2,1)S(1)} %whiten.2.own_ref, bf16[16,8,16,128]{3,2,1,0:T(8,128)(2,1)S(1)} %whiten.3.other_ref, bf16[2,128,1024]{2,1,0:T(8,128)(2,1)S(1)} %collective-permute-done.3.y13_ref, ...), custom_call_target="tpu_custom_call" | custom-call | tf_op jit(solution)/shard_map/second/pallas_call | solution.py:262
  (2 shorter events, 0.0 us)
Async XLA Ops:
  1.7 14.5 %collective-permute-start = (bf16[128,1024]{1,0:T(8,128)(2,1)S(1)}, bf16[128,1024]{1,0:T(8,128)(2,1)S(1)}, u32[]{:S(2)}, u32[]{:S(2)}) collective-permute-start(bf16[128,1024]{1,0:T(8,128)(2,1)S(1)} %normalize.1.x_ref), channel_id=1, source_target_pairs={{4,0},{5,1},{6,2},{7,3},{8,4},{9,5},{10,6},{11,7},{12,8},{13,9},{1... | collective-permute-start | bytes 786440 | tf_op jit(solution)/shard_map/ppermute | solution.py:213
  4.7 17.0 %collective-permute-start.2 = (bf16[128,1024]{1,0:T(8,128)(2,1)S(1)}, bf16[128,1024]{1,0:T(8,128)(2,1)S(1)}, u32[]{:S(2)}, u32[]{:S(2)}) collective-permute-start(bf16[128,1024]{1,0:T(8,128)(2,1)S(1)} %normalize.1.x_ref), channel_id=1, source_target_pairs={{1,0},{0,1},{3,2},{2,3},{5,4},{4,5},{7,6},{6,7},{9,8},{8,9},{11,10... | collective-permute-start | bytes 786440 | tf_op jit(solution)/shard_map/ppermute | solution.py:213
  16.2 8.4 %collective-permute-start.1 = (bf16[128,1024]{1,0:T(8,128)(2,1)S(1)}, bf16[128,1024]{1,0:T(8,128)(2,1)S(1)}, u32[]{:S(2)}, u32[]{:S(2)}) collective-permute-start(bf16[128,1024]{1,0:T(8,128)(2,1)S(1)} %collective-permute-done.y2_ref), channel_id=1, source_target_pairs={{1,0},{0,1},{3,2},{2,3},{5,4},{4,5},{7,6},{6,7},{9,8},{8,9},{11,10... | collective-permute-start | bytes 786440 | tf_op jit(solution)/shard_map/ppermute | solution.py:213
  18.2 11.4 %copy-start.1 = (s32[16,4,16]{2,1,0:T(4,128)S(1)}, s32[16,4,16]{2,1,0:T(4,128)}, u32[]{:S(2)}) copy-start(s32[16,4,16]{2,1,0:T(4,128)} %param.5) | copy-start | bytes 12292
  18.2 15.9 %copy-start = (s32[1,4]{1,0:T(1,128)S(1)}, s32[1,4]{1,0:T(1,128)}, u32[]{:S(2)}) copy-start(s32[1,4]{1,0:T(1,128)} %plan_ref.3) | copy-start | bytes 52
  18.2 15.9 %collective-permute-start.4 = (bf16[2,128,1024]{2,1,0:T(8,128)(2,1)S(1)}, bf16[2,128,1024]{2,1,0:T(8,128)(2,1)S(1)}, u32[]{:S(2)}, u32[]{:S(2)}) collective-permute-start(bf16[2,128,1024]{2,1,0:T(8,128)(2,1)S(1)} %pad_maximum_fusion.1), channel_id=1, source_target_pairs={{2,0},{3,1},{4,2},{5,3},{6,4},{7,5},{8,6},{9,7},{10,8},{11,9},{12,... | collective-permute-start | bytes 1572872 | tf_op jit(solution)/shard_map/ppermute | solution.py:213
  25.4 17.2 %collective-permute-start.3 = (bf16[2,128,1024]{2,1,0:T(8,128)(2,1)}, bf16[2,128,1024]{2,1,0:T(8,128)(2,1)S(1)}, u32[]{:S(2)}, u32[]{:S(2)}) collective-permute-start(bf16[2,128,1024]{2,1,0:T(8,128)(2,1)} %pad_maximum_fusion), channel_id=1, source_target_pairs={{2,0},{3,1},{4,2},{5,3},{6,4},{7,5},{8,6},{9,7},{10,8},{11,9},{12,... | collective-permute-start | bytes 1572872 | tf_op jit(solution)/shard_map/ppermute | solution.py:213
where the time goes:
time: 52.5 us; the launch traced here: 52.2 us
  Pallas kernels  25.4 us (48%)
  starting transfers between devices  14.9 us (28%)
  waiting for transfers between devices  10.6 us (20%)
  other arithmetic  0.9 us (2%)
    pallas_call x2, Pallas kernels, half_sums(): pl.pallas_call(functools.partial(half_kernel, half, per_row, second, scal...  17.9 us
    ppermute x5, starting transfers between devices, send(): return lax.ppermute(array, ('blk', 'seg'), pairs)  14.9 us
    ppermute x5, waiting for transfers between devices, send(): return lax.ppermute(array, ('blk', 'seg'), pairs)  10.6 us
    pallas_call x2, Pallas kernels, whiten(): pl.pallas_call(functools.partial(whiten_kernel, half), out_shape=jax.Shap...  5.85 us
    pallas_call x1, Pallas kernels, per_device(): pl.pallas_call(functools.partial(normalize_kernel, half), out_shape=jax.S...  1.68 us
  transfers between devices with their start and end apart: 5, of which 2 were waited for; matrix products, arithmetic and copies ran while one was open for 2% of the time, Pallas kernels for 28%

commit v1 on v0

v1 whole, which is shorter than its diff:
```python
import functools
import math

import jax
import jax.numpy as jnp
import ml_dtypes
import numpy as np
from jax import lax
from jax.experimental import pallas as pl
from jax.experimental.pallas import tpu as pltpu
from jax.sharding import PartitionSpec as P


EPS = 1e-05
TINY = 1e-30
STEPS = 4
F32 = jnp.float32
BF16 = jnp.bfloat16
VMEM = pl.BlockSpec(memory_space=pltpu.VMEM)
SMEM = pl.BlockSpec(memory_space=pltpu.SMEM)
HBM = pl.BlockSpec(memory_space=pltpu.HBM)
WIDTH = 256
REACH = 128


def angle_table(rows, cols, length):
    product = np.arange(rows)[:, None] * np.arange(cols)[None, :] % (2 * length)
    return product.astype(np.float32) * np.float32(math.pi / length)


def wave_table(length):
    angles = angle_table(length // 2, length, length)
    return np.stack((np.cos(angles), np.sin(angles))).astype(ml_dtypes.bfloat16)


def fill_box(box_ref, half):
    left = lax.broadcasted_iota(jnp.int32, box_ref.shape, 0) - REACH
    right = lax.broadcasted_iota(jnp.int32, box_ref.shape, 1)
    box_ref[...] = jnp.where(jnp.abs(left - right) <= half, 1.0, 0.0).astype(BF16)


def box_sum(values, box, col):
    low = max(0, col - REACH)
    high = min(values.shape[1], col + WIDTH + REACH)
    tile = box[low - col + REACH : high - col + REACH, :]
    return jnp.dot(values[:, low:high], tile, preferred_element_type=F32)


def normalize_kernel(half, wins, traces_hbm, out_ref, traces_ref, mag_ref, box_ref, sems):
    rows, length = traces_ref.shape
    chans = rows // wins
    copies = []
    for q, col in enumerate(range(0, length, WIDTH)):
        cols = slice(col, col + WIDTH)
        copies.append(pltpu.make_async_copy(traces_hbm.at[:, cols], traces_ref.at[:, cols], sems.at[q]))
        copies[-1].start()
    fill_box(box_ref, half)
    target = lax.broadcasted_iota(jnp.int32, (rows, rows), 0)
    source = lax.broadcasted_iota(jnp.int32, (rows, rows), 1)
    order = jnp.where(target % chans * wins + target // chans == source, 1.0, 0.0).astype(BF16)
    for q in range(len(copies) + 1):
        if q < len(copies):
            copies[q].wait()
            cols = slice(q * WIDTH, (q + 1) * WIDTH)
            mag_ref[:, cols] = jnp.abs(traces_ref[:, cols]).astype(BF16)
        if q > 0:
            cols = slice((q - 1) * WIDTH, q * WIDTH)
            level = box_sum(mag_ref, box_ref, (q - 1) * WIDTH) / (2 * half + 1)
            normed = (traces_ref[:, cols] / (level + EPS)).astype(BF16)
            out_ref[:, cols] = jnp.dot(order, normed, preferred_element_type=F32).astype(BF16)


def start_tables(wave_hbm, wave_ref, sems):
    copies = []
    for q, col in enumerate(range(0, wave_ref.shape[2], WIDTH)):
        cols = slice(col, col + WIDTH)
        copies.append(pltpu.make_async_copy(wave_hbm.at[:, :, cols], wave_ref.at[:, :, cols], sems.at[q]))
        copies[-1].start()
    return copies


def whiten_into(x_refs, wave_ref, box_ref, amp_ref, work_ref, out_refs, half, copies):
    rows, length = x_refs[0].shape
    count = len(x_refs)
    mid = length // 2
    shape = out_refs[0].shape[1:3] + (WIDTH,)
    both = jnp.concatenate([ref[:, :mid] for ref in x_refs] + [ref[:, mid:] for ref in x_refs], axis=0)
    lane = lax.broadcasted_iota(jnp.int32, (1, WIDTH), 1)
    even = (lane & 1) == 0
    sign = (1 - (lane & 2)).astype(F32)
    top = count * rows
    for q, col in enumerate(range(0, length, WIDTH)):
        cols = slice(col, col + WIDTH)
        copies[q].wait()
        cos_part = jnp.dot(both, wave_ref[0, :, cols], preferred_element_type=F32)
        sin_part = jnp.dot(both, wave_ref[1, :, cols], preferred_element_type=F32)
        re = cos_part[:top] + sign * jnp.where(even, cos_part[top:], -sin_part[top:])
        im = sin_part[:top] + sign * jnp.where(even, sin_part[top:], cos_part[top:])
        work_ref[0, :, cols] = re
        work_ref[1, :, cols] = im
        power = re * re + im * im
        amp_ref[:, cols] = (power * lax.rsqrt(jnp.maximum(power, TINY))).astype(BF16)
    for col in range(0, length, WIDTH):
        cols = slice(col, col + WIDTH)
        smooth = box_sum(amp_ref, box_ref, col) / (2 * half + 1)
        scale = 1.0 / (smooth + EPS)
        for c in range(2):
            white = work_ref[c, :, cols] * scale
            for n, ref in enumerate(out_refs):
                ref[c, :, :, cols] = white[n * rows : (n + 1) * rows].astype(ref.dtype).reshape(shape)


def whiten_kernel(half, x_ref, wave_hbm, out_ref, wave_ref, box_ref, amp_ref, work_ref, sems):
    copies = start_tables(wave_hbm, wave_ref, sems)
    fill_box(box_ref, half)
    whiten_into([x_ref], wave_ref, box_ref, amp_ref, work_ref, [out_ref], half, copies)


def cross_sums(mine_ref, far_ref, cross_ref, base):
    _, wins, chans, length = mine_ref.shape
    group = 8
    groups = chans // group

    def step(at, carry):
        lanes = pl.ds(pl.multiple_of(at // groups * 128, 128), 128)
        first = pl.multiple_of(at % groups * group, group)

        def add(w, sums):
            sums = list(sums)
            for c in range(2):
                far = far_ref[c, w, :, lanes]
                mine = mine_ref.at[c, w, pl.ds(first, group), lanes]
                for i in range(group):
                    sums[i] = sums[i] + mine[i : i + 1, :] * far
            return tuple(sums)

        zeros = tuple(jnp.zeros((chans, 128), F32) for _ in range(group))
        sums = lax.fori_loop(0, wins, add, zeros, unroll=8)
        total = jnp.concatenate(sums, axis=0).astype(BF16)
        cross_ref[pl.ds(base + pl.multiple_of(first * chans, group * chans), group * chans), lanes] = total
        return carry

    lax.fori_loop(0, length // 128 * groups, step, 0)


def flip_of(distance, per_row):
    blk = lax.axis_index("blk")
    chip = blk // 2
    core = blk % 2
    wrap = (chip % per_row == per_row - 1).astype(jnp.int32)
    ahead = ((chip + 1) % per_row == per_row - 1).astype(jnp.int32)
    one = jnp.where(core == 0, 0, wrap)
    three = jnp.where(core == 0, wrap, jnp.bitwise_xor(wrap, ahead))
    return jnp.where(distance == 1, one, jnp.where(distance == 2, wrap, jnp.where(distance == 3, three, 0)))


def half_kernel(
    half, per_row, second, scale, plan_ref, own_ref, other_ref, y1_ref, y2_ref, y3_ref, wave_hbm, *refs
):
    if second:
        part_ref, mask_ref, out_ref = refs[:3]
        refs = refs[3:]
    else:
        out_ref = refs[0]
        refs = refs[1:]
    wave_ref, box_ref, amp_ref, x_ref, work_ref, mine_ref, far_ref, cross_ref, sems = refs
    copies = start_tables(wave_hbm, wave_ref, sems)
    fill_box(box_ref, half)
    seg = lax.axis_index("seg")
    chans = own_ref.shape[2]
    wins = own_ref.shape[1]
    steps = out_ref.shape[0]
    pairs = chans * chans
    distances = [plan_ref[0, seg * steps + n] for n in range(steps)]

    for n, distance in enumerate(distances):
        which = jnp.bitwise_xor(flip_of(distance, per_row), second)
        for h, ref in enumerate((own_ref, other_ref)):

            @pl.when(which == h)
            def _(ref=ref, n=n):
                for c in range(2):
                    for w in range(wins):
                        mine_ref[n, c, w] = ref[c, w].astype(F32)

        for when, y_ref in ((distance == 1, y1_ref), (distance % 2 == 0, y2_ref), (distance == 3, y3_ref)):

            @pl.when(when)
            def _(y_ref=y_ref, n=n):
                x_ref[n] = y_ref[...]

    x_refs = [x_ref.at[n] for n in range(steps)]
    far_refs = [far_ref.at[n] for n in range(steps)]
    whiten_into(x_refs, wave_ref, box_ref, amp_ref, work_ref, far_refs, half, copies)

    for n, distance in enumerate(distances):

        @pl.when(distance == 0)
        def _(n=n):
            far_ref[n] = mine_ref[n]

        cross_sums(mine_ref.at[n], far_ref.at[n], cross_ref, n * pairs)

    lane = lax.broadcasted_iota(jnp.int32, (1, 128), 1)
    cross_ref[:, :128] = cross_ref[:, :128] * jnp.where(lane == 0, 0.5, 1.0).astype(BF16)
    folded = lax.dot_general(
        cross_ref[...], wave_ref[0], (((1,), (1,)), ((), ())), preferred_element_type=F32
    )
    for n, distance in enumerate(distances):
        rows = slice(n * pairs, (n + 1) * pairs)
        if second:
            keep = mask_ref[distance]
            for col in range(0, folded.shape[1], 128):
                cols = slice(col, col + 128)
                part = folded[rows, cols] * (2.0 * scale) + part_ref[n, :, cols]
                part = part * keep
                out_ref[n, :, cols] = part.astype(BF16)
        else:
            out_ref[n] = folded[rows] * (2.0 * scale)


def per_device(per_row, traces, mask, plan):
    chans, wins, length = traces.shape
    half = length // 16
    lags = length // 2
    rows = chans * wins
    blocks = lax.axis_size("blk")
    segs = lax.axis_size("seg")
    steps = STEPS // segs

    def send(array, source):
        pairs = []
        for b in range(blocks):
            for s in range(segs):
                where = source(b, s)
                if where is not None and where[0] < blocks:
                    pairs.append((where[0] * segs + where[1], b * segs + s))
        return lax.ppermute(array, ("blk", "seg"), pairs)

    def ahead(b, s, by):
        chip = b // 2
        wraps = (chip % per_row == per_row - 1) and (b + by) // 2 > chip
        return (b + by, 1 - s if wraps else s)

    def in_hbm(array):
        return pltpu.with_memory_space_constraint(array, pltpu.HBM)

    wave_tab = in_hbm(jnp.asarray(wave_table(length)))
    white_shape = (2, wins, chans, length)
    scale = 1.0 / math.sqrt(wins * segs * length)
    quarters = length // WIDTH
    box = pltpu.VMEM((WIDTH + 2 * REACH, WIDTH), BF16)
    wave = pltpu.VMEM(wave_tab.shape, BF16)
    amp = pltpu.VMEM((rows, length), BF16)
    work = pltpu.VMEM((2, rows, length), F32)

    x = pl.pallas_call(
        functools.partial(normalize_kernel, half, wins),
        out_shape=jax.ShapeDtypeStruct((rows, length), BF16),
        in_specs=[HBM],
        out_specs=VMEM,
        scratch_shapes=[
            pltpu.VMEM((rows, length), F32),
            amp,
            box,
            pltpu.SemaphoreType.DMA((quarters,)),
        ],
        compiler_params=pltpu.CompilerParams(vmem_limit_bytes=6 << 20),
        name="normalize",
    )(in_hbm(traces.reshape(rows, length)))

    def whiten(array):
        return pl.pallas_call(
            functools.partial(whiten_kernel, half),
            out_shape=jax.ShapeDtypeStruct(white_shape, BF16),
            in_specs=[VMEM, HBM],
            out_specs=VMEM,
            scratch_shapes=[wave, box, amp, work, pltpu.SemaphoreType.DMA((quarters,))],
            compiler_params=pltpu.CompilerParams(vmem_limit_bytes=12 << 20),
            name="whiten",
        )(array, wave_tab)

    def half_sums(second, dtype, *args):
        return pl.pallas_call(
            functools.partial(half_kernel, half, per_row, second, scale),
            out_shape=jax.ShapeDtypeStruct((steps, chans * chans, lags), dtype),
            in_specs=[SMEM] + [VMEM] * 5 + [HBM] + [VMEM] * (2 * second),
            out_specs=VMEM,
            scratch_shapes=[
                wave,
                box,
                pltpu.VMEM((steps * rows, length), BF16),
                pltpu.VMEM((steps, rows, length), BF16),
                pltpu.VMEM((2, steps * rows, length), F32),
                pltpu.VMEM((steps,) + white_shape, F32),
                pltpu.VMEM((steps,) + white_shape, F32),
                pltpu.VMEM((steps * chans * chans, length), BF16),
                pltpu.SemaphoreType.DMA((quarters,)),
            ],
            compiler_params=pltpu.CompilerParams(vmem_limit_bytes=24 << 20),
            name="second" if second else "first",
        )(plan, own, other, *args)

    keep = jnp.transpose(mask, (1, 0, 2)).reshape(STEPS, chans * chans, 1)
    keep = jnp.broadcast_to(keep, (STEPS, chans * chans, 128)).astype(F32)

    def next_block(b, s):
        return ahead(b, s, 1) if b % 2 else (b + 1, s)

    y2 = send(x, lambda b, s: ahead(b, s, 2))
    o = send(x, lambda b, s: (b, 1 - s))
    y1 = send(x, next_block)
    own = whiten(x)
    y2, own = lax.optimization_barrier((y2, own))
    y2o = send(y2, lambda b, s: (b, 1 - s))
    y3 = send(y2, next_block)
    other = whiten(o)
    y2o, other = lax.optimization_barrier((y2o, other))
    y13o = send(jnp.stack((o, y2o)), next_block)
    part = half_sums(0, F32, y1, y2, y3, wave_tab)
    out = half_sums(1, BF16, y13o[0], y2o, y13o[1], wave_tab, part, keep)
    return out.reshape(steps, chans, chans, lags)


def solution(mesh):
    def body(traces, mask, plan):
        return per_device(8, traces, mask, plan)

    return jax.shard_map(
        body,
        mesh=mesh,
        in_specs=(P("blk", "seg", None), P("blk", None, None), P("blk", None)),
        out_specs=P("seg", "blk", None, None),
        check_vma=False,
    )
```

time: 52.5 us -> 64.5 us (1.23)
  waiting for transfers between devices: 10.6 us -> 23.3 us
  other arithmetic: 0.9 us -> 0.06 us
    ppermute x5 -> x6, waiting for transfers between devices: 10.6 us -> 23.3 us  [send(): return lax.ppermute(array, ('blk', 'seg'), pairs)]
    another operation x1, other arithmetic: 0.84 us -> 0.05 us  [per_device(): y13o = send(jnp.stack((o, y2o)), next_block)]
    pallas_call x2, Pallas kernels: 17.9 us -> 17.2 us  [half_sums(): pl.pallas_call(functools.partial(half_kernel, half, per_row, second, scal...]
    pallas_call x1, Pallas kernels: 1.68 us -> 2.34 us  [per_device(): pl.pallas_call(functools.partial(normalize_kernel, half, wins), out_shape...]
    ppermute x5 -> x6, starting transfers between devices: 14.9 us -> 15.5 us  [send(): return lax.ppermute(array, ('blk', 'seg'), pairs)]
  transfers between devices with their start and end apart: 5 -> 6, of which waited for: 2 -> 4; matrix products, arithmetic and copies ran while one was open for 2% -> 0% of each run, Pallas kernels for 28% -> 21%
where the time goes in v1:
time: 64.5 us; the launch traced here: 64.2 us
  Pallas kernels  24.9 us (39%)
  waiting for transfers between devices  23.3 us (36%)
  starting transfers between devices  15.5 us (24%)
    ppermute x6, waiting for transfers between devices, send(): return lax.ppermute(array, ('blk', 'seg'), pairs)  23.3 us
    pallas_call x2, Pallas kernels, half_sums(): pl.pallas_call(functools.partial(half_kernel, half, per_row, second, scal...  17.2 us
    ppermute x6, starting transfers between devices, send(): return lax.ppermute(array, ('blk', 'seg'), pairs)  15.5 us
    pallas_call x2, Pallas kernels, whiten(): pl.pallas_call(functools.partial(whiten_kernel, half), out_shape=jax.Shap...  5.29 us
    pallas_call x1, Pallas kernels, per_device(): pl.pallas_call(functools.partial(normalize_kernel, half, wins), out_shape...  2.34 us
  transfers between devices with their start and end apart: 6, of which 4 were waited for; matrix products, arithmetic and copies ran while one was open for 0% of the time, Pallas kernels for 21%

profile of v1, /device:TPU:255, one launch (start us, length us, event | category | flops | bytes accessed | tf_op | source)
XLA Modules:
  0.0 64.2 jit_solution(11342907439361985013)
XLA Ops:
  0.0 2.3 %normalize.1.x_ref = bf16[128,1024]{1,0:T(8,128)(2,1)S(1)} custom-call(f32[128,1024]{1,0:T(8,128)} %bitcast.12), custom_call_target="tpu_custom_call" | custom-call | tf_op jit(solution)/shard_map/normalize/pallas_call | solution.py:257
  2.3 3.0 %collective-permute-start = (bf16[128,1024]{1,0:T(8,128)(2,1)S(1)}, bf16[128,1024]{1,0:T(8,128)(2,1)S(1)}, u32[]{:S(2)}, u32[]{:S(2)}) collective-permute-start(bf16[128,1024]{1,0:T(8,128)(2,1)S(1)} %normalize.1.x_ref), channel_id=1, source_target_pairs={{4,0},{5,1},{6,2},{7,3},{8,4},{9,5},{10,6},{11,7},{12,8},{13,9},{1... | collective-permute-start | bytes 786440 | tf_op jit(solution)/shard_map/ppermute | solution.py:238
  5.3 2.5 %collective-permute-start.2 = (bf16[128,1024]{1,0:T(8,128)(2,1)S(1)}, bf16[128,1024]{1,0:T(8,128)(2,1)S(1)}, u32[]{:S(2)}, u32[]{:S(2)}) collective-permute-start(bf16[128,1024]{1,0:T(8,128)(2,1)S(1)} %normalize.1.x_ref), channel_id=1, source_target_pairs={{1,0},{0,1},{3,2},{2,3},{5,4},{4,5},{7,6},{6,7},{9,8},{8,9},{11,10... | collective-permute-start | bytes 786440 | tf_op jit(solution)/shard_map/ppermute | solution.py:238
  7.8 2.6 %whiten.2.own_ref = bf16[2,8,16,1024]{3,2,1,0:T(8,128)(2,1)S(1)} custom-call(bf16[128,1024]{1,0:T(8,128)(2,1)S(1)} %normalize.1.x_ref, bf16[2,512,1024]{2,1,0:T(8,128)(2,1)} %constant.2.clone.wave_hbm), custom_call_target="tpu_custom_call" | custom-call | tf_op jit(solution)/shard_map/whiten/pallas_call | solution.py:273
  10.4 0.0 copy-start.1
  10.5 0.0 copy-start
  10.5 6.4 %collective-permute-done.y2_ref = bf16[128,1024]{1,0:T(8,128)(2,1)S(1)} collective-permute-done((bf16[128,1024]{1,0:T(8,128)(2,1)S(1)}, bf16[128,1024]{1,0:T(8,128)(2,1)S(1)}, u32[]{:S(2)}, u32[]{:S(2)}) %collective-permute-start) | collective-permute-done | bytes 262176 | tf_op jit(solution)/shard_map/ppermute | solution.py:238
  16.9 1.9 %collective-permute-start.1 = (bf16[128,1024]{1,0:T(8,128)(2,1)S(1)}, bf16[128,1024]{1,0:T(8,128)(2,1)S(1)}, u32[]{:S(2)}, u32[]{:S(2)}) collective-permute-start(bf16[128,1024]{1,0:T(8,128)(2,1)S(1)} %collective-permute-done.y2_ref), channel_id=1, source_target_pairs={{1,0},{0,1},{3,2},{2,3},{5,4},{4,5},{7,6},{6,7},{9,8},{8,9},{11,10... | collective-permute-start | bytes 786440 | tf_op jit(solution)/shard_map/ppermute | solution.py:238
  18.8 0.0 collective-permute-done.2.x_ref
  18.8 2.6 %whiten.3.other_ref = bf16[2,8,16,1024]{3,2,1,0:T(8,128)(2,1)S(1)} custom-call(bf16[128,1024]{1,0:T(8,128)(2,1)S(1)} %collective-permute-done.2.x_ref, bf16[2,512,1024]{2,1,0:T(8,128)(2,1)} %constant.2.clone.wave_hbm), custom_call_target="tpu_custom_call" | custom-call | tf_op jit(solution)/shard_map/whiten/pallas_call | solution.py:273
  21.4 3.6 %collective-permute-done.1.y2_ref = bf16[128,1024]{1,0:T(8,128)(2,1)S(1)} collective-permute-done((bf16[128,1024]{1,0:T(8,128)(2,1)S(1)}, bf16[128,1024]{1,0:T(8,128)(2,1)S(1)}, u32[]{:S(2)}, u32[]{:S(2)}) %collective-permute-start.1) | collective-permute-done | bytes 262176 | tf_op jit(solution)/shard_map/ppermute | solution.py:238
  25.1 0.1 pad_maximum_fusion
  25.1 4.3 %collective-permute-start.3 = (bf16[2,128,1024]{2,1,0:T(8,128)(2,1)S(1)}, bf16[2,128,1024]{2,1,0:T(8,128)(2,1)S(1)}, u32[]{:S(2)}, u32[]{:S(2)}) collective-permute-start(bf16[2,128,1024]{2,1,0:T(8,128)(2,1)S(1)} %pad_maximum_fusion), channel_id=1, source_target_pairs={{2,0},{3,1},{4,2},{5,3},{6,4},{7,5},{8,6},{9,7},{10,8},{11,9},{12,... | collective-permute-start | bytes 1572872 | tf_op jit(solution)/shard_map/ppermute | solution.py:238
  29.4 1.9 %collective-permute-start.4 = (bf16[128,1024]{1,0:T(8,128)(2,1)S(1)}, bf16[128,1024]{1,0:T(8,128)(2,1)S(1)}, u32[]{:S(2)}, u32[]{:S(2)}) collective-permute-start(bf16[128,1024]{1,0:T(8,128)(2,1)S(1)} %normalize.1.x_ref), channel_id=1, source_target_pairs={{2,0},{3,1},{4,2},{5,3},{6,4},{7,5},{8,6},{9,7},{10,8},{11,9},{12,... | collective-permute-start | bytes 786440 | tf_op jit(solution)/shard_map/ppermute | solution.py:238
  31.4 1.9 %collective-permute-start.5 = (bf16[128,1024]{1,0:T(8,128)(2,1)S(1)}, bf16[128,1024]{1,0:T(8,128)(2,1)S(1)}, u32[]{:S(2)}, u32[]{:S(2)}) collective-permute-start(bf16[128,1024]{1,0:T(8,128)(2,1)S(1)} %collective-permute-done.y2_ref), channel_id=1, source_target_pairs={{2,0},{3,1},{4,2},{5,3},{6,4},{7,5},{8,6},{9,7},{10,8},{11,9},{12,... | collective-permute-start | bytes 786440 | tf_op jit(solution)/shard_map/ppermute | solution.py:238
  33.3 0.0 copy-done.1
  33.3 0.1 convert_element_type.9
  33.4 10.5 %collective-permute-done.4.y1_ref = bf16[128,1024]{1,0:T(8,128)(2,1)S(1)} collective-permute-done((bf16[128,1024]{1,0:T(8,128)(2,1)S(1)}, bf16[128,1024]{1,0:T(8,128)(2,1)S(1)}, u32[]{:S(2)}, u32[]{:S(2)}) %collective-permute-start.4) | collective-permute-done | bytes 262176 | tf_op jit(solution)/shard_map/ppermute | solution.py:238
  43.9 2.8 %collective-permute-done.5.y3_ref = bf16[128,1024]{1,0:T(8,128)(2,1)S(1)} collective-permute-done((bf16[128,1024]{1,0:T(8,128)(2,1)S(1)}, bf16[128,1024]{1,0:T(8,128)(2,1)S(1)}, u32[]{:S(2)}, u32[]{:S(2)}) %collective-permute-start.5) | collective-permute-done | bytes 262176 | tf_op jit(solution)/shard_map/ppermute | solution.py:238
  46.7 0.0 copy-done
  46.7 8.2 %first.1.refs_0_ = f32[2,256,512]{2,1,0:T(8,128)S(1)} custom-call(s32[1,4]{1,0:T(1,128)S(1)} %copy-done, bf16[2,8,16,1024]{3,2,1,0:T(8,128)(2,1)S(1)} %whiten.2.own_ref, bf16[2,8,16,1024]{3,2,1,0:T(8,128)(2,1)S(1)} %whiten.3.other_ref, bf16[128,1024]{1,0:T(8,128)(2,1)S(1)} %collective-permute-done.4.y1_ref, ...), custom_call_target="tpu_custom_call" | custom-call | tf_op jit(solution)/shard_map/first/pallas_call | solution.py:284
  54.9 0.0 collective-permute-done.3
  55.0 0.2 broadcast_in_dim.2.refs_1_
  55.1 9.0 %second.1 = bf16[2,256,512]{2,1,0:T(8,128)(2,1)} custom-call(s32[1,4]{1,0:T(1,128)S(1)} %copy-done, bf16[2,8,16,1024]{3,2,1,0:T(8,128)(2,1)S(1)} %whiten.2.own_ref, bf16[2,8,16,1024]{3,2,1,0:T(8,128)(2,1)S(1)} %whiten.3.other_ref, bf16[128,1024]{1,0:T(8,128)(2,1)S(1)} %get-tuple-element.14.y1_ref, bf16[128,1024]{1,0:T(8,128)(2,1)S(1)} %collective-permute-done.1.y2_ref, ...), custom_call_target="tpu_custom_call" | custom-call | tf_op jit(solution)/shard_map/second/pallas_call | solution.py:284
  (3 shorter events, 0.0 us)
Async XLA Ops:
  2.3 14.5 %collective-permute-start = (bf16[128,1024]{1,0:T(8,128)(2,1)S(1)}, bf16[128,1024]{1,0:T(8,128)(2,1)S(1)}, u32[]{:S(2)}, u32[]{:S(2)}) collective-permute-start(bf16[128,1024]{1,0:T(8,128)(2,1)S(1)} %normalize.1.x_ref), channel_id=1, source_target_pairs={{4,0},{5,1},{6,2},{7,3},{8,4},{9,5},{10,6},{11,7},{12,8},{13,9},{1... | collective-permute-start | bytes 786440 | tf_op jit(solution)/shard_map/ppermute | solution.py:238
  5.3 13.5 %collective-permute-start.2 = (bf16[128,1024]{1,0:T(8,128)(2,1)S(1)}, bf16[128,1024]{1,0:T(8,128)(2,1)S(1)}, u32[]{:S(2)}, u32[]{:S(2)}) collective-permute-start(bf16[128,1024]{1,0:T(8,128)(2,1)S(1)} %normalize.1.x_ref), channel_id=1, source_target_pairs={{1,0},{0,1},{3,2},{2,3},{5,4},{4,5},{7,6},{6,7},{9,8},{8,9},{11,10... | collective-permute-start | bytes 786440 | tf_op jit(solution)/shard_map/ppermute | solution.py:238
  10.4 22.8 %copy-start.1 = (s32[16,4,16]{2,1,0:T(4,128)S(1)}, s32[16,4,16]{2,1,0:T(4,128)}, u32[]{:S(2)}) copy-start(s32[16,4,16]{2,1,0:T(4,128)} %param.5) | copy-start | bytes 12292
  10.5 36.2 %copy-start = (s32[1,4]{1,0:T(1,128)S(1)}, s32[1,4]{1,0:T(1,128)}, u32[]{:S(2)}) copy-start(s32[1,4]{1,0:T(1,128)} %plan_ref.3) | copy-start | bytes 52
  16.9 8.2 %collective-permute-start.1 = (bf16[128,1024]{1,0:T(8,128)(2,1)S(1)}, bf16[128,1024]{1,0:T(8,128)(2,1)S(1)}, u32[]{:S(2)}, u32[]{:S(2)}) collective-permute-start(bf16[128,1024]{1,0:T(8,128)(2,1)S(1)} %collective-permute-done.y2_ref), channel_id=1, source_target_pairs={{1,0},{0,1},{3,2},{2,3},{5,4},{4,5},{7,6},{6,7},{9,8},{8,9},{11,10... | collective-permute-start | bytes 786440 | tf_op jit(solution)/shard_map/ppermute | solution.py:238
  25.1 29.8 %collective-permute-start.3 = (bf16[2,128,1024]{2,1,0:T(8,128)(2,1)S(1)}, bf16[2,128,1024]{2,1,0:T(8,128)(2,1)S(1)}, u32[]{:S(2)}, u32[]{:S(2)}) collective-permute-start(bf16[2,128,1024]{2,1,0:T(8,128)(2,1)S(1)} %pad_maximum_fusion), channel_id=1, source_target_pairs={{2,0},{3,1},{4,2},{5,3},{6,4},{7,5},{8,6},{9,7},{10,8},{11,9},{12,... | collective-permute-start | bytes 1572872 | tf_op jit(solution)/shard_map/ppermute | solution.py:238
  29.4 14.4 %collective-permute-start.4 = (bf16[128,1024]{1,0:T(8,128)(2,1)S(1)}, bf16[128,1024]{1,0:T(8,128)(2,1)S(1)}, u32[]{:S(2)}, u32[]{:S(2)}) collective-permute-start(bf16[128,1024]{1,0:T(8,128)(2,1)S(1)} %normalize.1.x_ref), channel_id=1, source_target_pairs={{2,0},{3,1},{4,2},{5,3},{6,4},{7,5},{8,6},{9,7},{10,8},{11,9},{12,... | collective-permute-start | bytes 786440 | tf_op jit(solution)/shard_map/ppermute | solution.py:238
  31.4 15.3 %collective-permute-start.5 = (bf16[128,1024]{1,0:T(8,128)(2,1)S(1)}, bf16[128,1024]{1,0:T(8,128)(2,1)S(1)}, u32[]{:S(2)}, u32[]{:S(2)}) collective-permute-start(bf16[128,1024]{1,0:T(8,128)(2,1)S(1)} %collective-permute-done.y2_ref), channel_id=1, source_target_pairs={{2,0},{3,1},{4,2},{5,3},{6,4},{7,5},{8,6},{9,7},{10,8},{11,9},{12,... | collective-permute-start | bytes 786440 | tf_op jit(solution)/shard_map/ppermute | solution.py:238

commit v2 on v1

--- a/solution.py
+++ b/solution.py
@@ -21,6 +21,7 @@
 HBM = pl.BlockSpec(memory_space=pltpu.HBM)
 WIDTH = 256
 REACH = 128
+PARTS = 2
 
 
 def angle_table(rows, cols, length):
@@ -30,7 +31,8 @@
 
 def wave_table(length):
     angles = angle_table(length // 2, length, length)
-    return np.stack((np.cos(angles), np.sin(angles))).astype(ml_dtypes.bfloat16)
+    table = np.stack((np.cos(angles), np.sin(angles))).astype(ml_dtypes.bfloat16)
+    return np.stack(np.split(table, PARTS, axis=2))
 
 
 def fill_box(box_ref, half):
@@ -71,11 +73,9 @@
 
 
 def start_tables(wave_hbm, wave_ref, sems):
-    copies = []
-    for q, col in enumerate(range(0, wave_ref.shape[2], WIDTH)):
-        cols = slice(col, col + WIDTH)
-        copies.append(pltpu.make_async_copy(wave_hbm.at[:, :, cols], wave_ref.at[:, :, cols], sems.at[q]))
-        copies[-1].start()
+    copies = [pltpu.make_async_copy(wave_hbm.at[q], wave_ref.at[q], sems.at[q]) for q in range(PARTS)]
+    for copy in copies:
+        copy.start()
     return copies
 
 
@@ -89,11 +89,13 @@
     even = (lane & 1) == 0
     sign = (1 - (lane & 2)).astype(F32)
     top = count * rows
-    for q, col in enumerate(range(0, length, WIDTH)):
+    for col in range(0, length, WIDTH):
         cols = slice(col, col + WIDTH)
-        copies[q].wait()
-        cos_part = jnp.dot(both, wave_ref[0, :, cols], preferred_element_type=F32)
-        sin_part = jnp.dot(both, wave_ref[1, :, cols], preferred_element_type=F32)
+        q, at = divmod(col, length // PARTS)
+        if at == 0:
+            copies[q].wait()
+        cos_part = jnp.dot(both, wave_ref[q, 0, :, at : at + WIDTH], preferred_element_type=F32)
+        sin_part = jnp.dot(both, wave_ref[q, 1, :, at : at + WIDTH], preferred_element_type=F32)
         re = cos_part[:top] + sign * jnp.where(even, cos_part[top:], -sin_part[top:])
         im = sin_part[:top] + sign * jnp.where(even, sin_part[top:], cos_part[top:])
         work_ref[0, :, cols] = re
@@ -204,7 +206,7 @@
     lane = lax.broadcasted_iota(jnp.int32, (1, 128), 1)
     cross_ref[:, :128] = cross_ref[:, :128] * jnp.where(lane == 0, 0.5, 1.0).astype(BF16)
     folded = lax.dot_general(
-        cross_ref[...], wave_ref[0], (((1,), (1,)), ((), ())), preferred_element_type=F32
+        cross_ref[...], jnp.concatenate([wave_ref[q, 0] for q in range(PARTS)], axis=1), (((1,), (1,)), ((), ())), preferred_element_type=F32
     )
     for n, distance in enumerate(distances):
         rows = slice(n * pairs, (n + 1) * pairs)

time: 64.5 us -> 64 us (level)
  Pallas kernels: 24.9 us -> 23.8 us
  transfers between devices with their start and end apart: 6 -> 6, of which waited for: 4 -> 4; matrix products, arithmetic and copies ran while one was open for 0% -> 0% of each run, Pallas kernels for 21% -> 20%
where the time goes in v2:
time: 64 us; the launch traced here: 63.6 us
  Pallas kernels  23.8 us (37%)
  waiting for transfers between devices  23.7 us (37%)
  starting transfers between devices  15.5 us (24%)
    ppermute x6, waiting for transfers between devices, send(): return lax.ppermute(array, ('blk', 'seg'), pairs)  23.7 us
    pallas_call x2, Pallas kernels, half_sums(): pl.pallas_call(functools.partial(half_kernel, half, per_row, second, scal...  16.6 us
    ppermute x6, starting transfers between devices, send(): return lax.ppermute(array, ('blk', 'seg'), pairs)  15.5 us
    pallas_call x2, Pallas kernels, whiten(): pl.pallas_call(functools.partial(whiten_kernel, half), out_shape=jax.Shap...  4.86 us
    pallas_call x1, Pallas kernels, per_device(): pl.pallas_call(functools.partial(normalize_kernel, half, wins), out_shape...  2.34 us
  transfers between devices with their start and end apart: 6, of which 4 were waited for; matrix products, arithmetic and copies ran while one was open for 0% of the time, Pallas kernels for 20%

profile of v2, /device:TPU:255, one launch (start us, length us, event | category | flops | bytes accessed | tf_op | source)
XLA Modules:
  0.0 63.6 jit_solution(14865745758510711603)
XLA Ops:
  0.0 2.3 %normalize.1.x_ref = bf16[128,1024]{1,0:T(8,128)(2,1)S(1)} custom-call(f32[128,1024]{1,0:T(8,128)} %bitcast.12), custom_call_target="tpu_custom_call" | custom-call | tf_op jit(solution)/shard_map/normalize/pallas_call | solution.py:259
  2.3 3.0 %collective-permute-start = (bf16[128,1024]{1,0:T(8,128)(2,1)S(1)}, bf16[128,1024]{1,0:T(8,128)(2,1)S(1)}, u32[]{:S(2)}, u32[]{:S(2)}) collective-permute-start(bf16[128,1024]{1,0:T(8,128)(2,1)S(1)} %normalize.1.x_ref), channel_id=1, source_target_pairs={{4,0},{5,1},{6,2},{7,3},{8,4},{9,5},{10,6},{11,7},{12,8},{13,9},{1... | collective-permute-start | bytes 786440 | tf_op jit(solution)/shard_map/ppermute | solution.py:240
  5.3 2.5 %collective-permute-start.2 = (bf16[128,1024]{1,0:T(8,128)(2,1)S(1)}, bf16[128,1024]{1,0:T(8,128)(2,1)S(1)}, u32[]{:S(2)}, u32[]{:S(2)}) collective-permute-start(bf16[128,1024]{1,0:T(8,128)(2,1)S(1)} %normalize.1.x_ref), channel_id=1, source_target_pairs={{1,0},{0,1},{3,2},{2,3},{5,4},{4,5},{7,6},{6,7},{9,8},{8,9},{11,10... | collective-permute-start | bytes 786440 | tf_op jit(solution)/shard_map/ppermute | solution.py:240
  7.8 2.4 %whiten.2.own_ref = bf16[2,8,16,1024]{3,2,1,0:T(8,128)(2,1)S(1)} custom-call(bf16[128,1024]{1,0:T(8,128)(2,1)S(1)} %normalize.1.x_ref, bf16[2,2,512,512]{3,2,1,0:T(8,128)(2,1)} %constant.2.clone.wave_hbm), custom_call_target="tpu_custom_call" | custom-call | tf_op jit(solution)/shard_map/whiten/pallas_call | solution.py:275
  10.2 0.0 copy-start.1
  10.2 0.0 copy-start
  10.3 6.6 %collective-permute-done.y2_ref = bf16[128,1024]{1,0:T(8,128)(2,1)S(1)} collective-permute-done((bf16[128,1024]{1,0:T(8,128)(2,1)S(1)}, bf16[128,1024]{1,0:T(8,128)(2,1)S(1)}, u32[]{:S(2)}, u32[]{:S(2)}) %collective-permute-start) | collective-permute-done | bytes 262176 | tf_op jit(solution)/shard_map/ppermute | solution.py:240
  16.9 1.9 %collective-permute-start.1 = (bf16[128,1024]{1,0:T(8,128)(2,1)S(1)}, bf16[128,1024]{1,0:T(8,128)(2,1)S(1)}, u32[]{:S(2)}, u32[]{:S(2)}) collective-permute-start(bf16[128,1024]{1,0:T(8,128)(2,1)S(1)} %collective-permute-done.y2_ref), channel_id=1, source_target_pairs={{1,0},{0,1},{3,2},{2,3},{5,4},{4,5},{7,6},{6,7},{9,8},{8,9},{11,10... | collective-permute-start | bytes 786440 | tf_op jit(solution)/shard_map/ppermute | solution.py:240
  18.8 0.0 collective-permute-done.2.x_ref
  18.8 2.4 %whiten.3.other_ref = bf16[2,8,16,1024]{3,2,1,0:T(8,128)(2,1)S(1)} custom-call(bf16[128,1024]{1,0:T(8,128)(2,1)S(1)} %collective-permute-done.2.x_ref, bf16[2,2,512,512]{3,2,1,0:T(8,128)(2,1)} %constant.2.clone.wave_hbm), custom_call_target="tpu_custom_call" | custom-call | tf_op jit(solution)/shard_map/whiten/pallas_call | solution.py:275
  21.2 3.9 %collective-permute-done.1.y2_ref = bf16[128,1024]{1,0:T(8,128)(2,1)S(1)} collective-permute-done((bf16[128,1024]{1,0:T(8,128)(2,1)S(1)}, bf16[128,1024]{1,0:T(8,128)(2,1)S(1)}, u32[]{:S(2)}, u32[]{:S(2)}) %collective-permute-start.1) | collective-permute-done | bytes 262176 | tf_op jit(solution)/shard_map/ppermute | solution.py:240
  25.1 0.1 pad_maximum_fusion
  25.1 4.3 %collective-permute-start.3 = (bf16[2,128,1024]{2,1,0:T(8,128)(2,1)S(1)}, bf16[2,128,1024]{2,1,0:T(8,128)(2,1)S(1)}, u32[]{:S(2)}, u32[]{:S(2)}) collective-permute-start(bf16[2,128,1024]{2,1,0:T(8,128)(2,1)S(1)} %pad_maximum_fusion), channel_id=1, source_target_pairs={{2,0},{3,1},{4,2},{5,3},{6,4},{7,5},{8,6},{9,7},{10,8},{11,9},{12,... | collective-permute-start | bytes 1572872 | tf_op jit(solution)/shard_map/ppermute | solution.py:240
  29.4 1.9 %collective-permute-start.4 = (bf16[128,1024]{1,0:T(8,128)(2,1)S(1)}, bf16[128,1024]{1,0:T(8,128)(2,1)S(1)}, u32[]{:S(2)}, u32[]{:S(2)}) collective-permute-start(bf16[128,1024]{1,0:T(8,128)(2,1)S(1)} %normalize.1.x_ref), channel_id=1, source_target_pairs={{2,0},{3,1},{4,2},{5,3},{6,4},{7,5},{8,6},{9,7},{10,8},{11,9},{12,... | collective-permute-start | bytes 786440 | tf_op jit(solution)/shard_map/ppermute | solution.py:240
  31.4 1.9 %collective-permute-start.5 = (bf16[128,1024]{1,0:T(8,128)(2,1)S(1)}, bf16[128,1024]{1,0:T(8,128)(2,1)S(1)}, u32[]{:S(2)}, u32[]{:S(2)}) collective-permute-start(bf16[128,1024]{1,0:T(8,128)(2,1)S(1)} %collective-permute-done.y2_ref), channel_id=1, source_target_pairs={{2,0},{3,1},{4,2},{5,3},{6,4},{7,5},{8,6},{9,7},{10,8},{11,9},{12,... | collective-permute-start | bytes 786440 | tf_op jit(solution)/shard_map/ppermute | solution.py:240
  33.3 0.0 copy-done.1
  33.3 0.1 convert_element_type.9
  33.4 10.5 %collective-permute-done.4.y1_ref = bf16[128,1024]{1,0:T(8,128)(2,1)S(1)} collective-permute-done((bf16[128,1024]{1,0:T(8,128)(2,1)S(1)}, bf16[128,1024]{1,0:T(8,128)(2,1)S(1)}, u32[]{:S(2)}, u32[]{:S(2)}) %collective-permute-start.4) | collective-permute-done | bytes 262176 | tf_op jit(solution)/shard_map/ppermute | solution.py:240
  43.9 2.8 %collective-permute-done.5.y3_ref = bf16[128,1024]{1,0:T(8,128)(2,1)S(1)} collective-permute-done((bf16[128,1024]{1,0:T(8,128)(2,1)S(1)}, bf16[128,1024]{1,0:T(8,128)(2,1)S(1)}, u32[]{:S(2)}, u32[]{:S(2)}) %collective-permute-start.5) | collective-permute-done | bytes 262176 | tf_op jit(solution)/shard_map/ppermute | solution.py:240
  46.7 0.0 copy-done
  46.7 7.9 %first.1.refs_0_ = f32[2,256,512]{2,1,0:T(8,128)S(1)} custom-call(s32[1,4]{1,0:T(1,128)S(1)} %copy-done, bf16[2,8,16,1024]{3,2,1,0:T(8,128)(2,1)S(1)} %whiten.2.own_ref, bf16[2,8,16,1024]{3,2,1,0:T(8,128)(2,1)S(1)} %whiten.3.other_ref, bf16[128,1024]{1,0:T(8,128)(2,1)S(1)} %collective-permute-done.4.y1_ref, ...), custom_call_target="tpu_custom_call" | custom-call | tf_op jit(solution)/shard_map/first/pallas_call | solution.py:286
  54.6 0.0 collective-permute-done.3
  54.7 0.2 broadcast_in_dim.2.refs_1_
  54.9 8.7 %second.1 = bf16[2,256,512]{2,1,0:T(8,128)(2,1)} custom-call(s32[1,4]{1,0:T(1,128)S(1)} %copy-done, bf16[2,8,16,1024]{3,2,1,0:T(8,128)(2,1)S(1)} %whiten.2.own_ref, bf16[2,8,16,1024]{3,2,1,0:T(8,128)(2,1)S(1)} %whiten.3.other_ref, bf16[128,1024]{1,0:T(8,128)(2,1)S(1)} %get-tuple-element.14.y1_ref, bf16[128,1024]{1,0:T(8,128)(2,1)S(1)} %collective-permute-done.1.y2_ref, ...), custom_call_target="tpu_custom_call" | custom-call | tf_op jit(solution)/shard_map/second/pallas_call | solution.py:286
  (3 shorter events, 0.0 us)
Async XLA Ops:
  2.3 14.5 %collective-permute-start = (bf16[128,1024]{1,0:T(8,128)(2,1)S(1)}, bf16[128,1024]{1,0:T(8,128)(2,1)S(1)}, u32[]{:S(2)}, u32[]{:S(2)}) collective-permute-start(bf16[128,1024]{1,0:T(8,128)(2,1)S(1)} %normalize.1.x_ref), channel_id=1, source_target_pairs={{4,0},{5,1},{6,2},{7,3},{8,4},{9,5},{10,6},{11,7},{12,8},{13,9},{1... | collective-permute-start | bytes 786440 | tf_op jit(solution)/shard_map/ppermute | solution.py:240
  5.3 13.5 %collective-permute-start.2 = (bf16[128,1024]{1,0:T(8,128)(2,1)S(1)}, bf16[128,1024]{1,0:T(8,128)(2,1)S(1)}, u32[]{:S(2)}, u32[]{:S(2)}) collective-permute-start(bf16[128,1024]{1,0:T(8,128)(2,1)S(1)} %normalize.1.x_ref), channel_id=1, source_target_pairs={{1,0},{0,1},{3,2},{2,3},{5,4},{4,5},{7,6},{6,7},{9,8},{8,9},{11,10... | collective-permute-start | bytes 786440 | tf_op jit(solution)/shard_map/ppermute | solution.py:240
  10.2 23.1 %copy-start.1 = (s32[16,4,16]{2,1,0:T(4,128)S(1)}, s32[16,4,16]{2,1,0:T(4,128)}, u32[]{:S(2)}) copy-start(s32[16,4,16]{2,1,0:T(4,128)} %param.5) | copy-start | bytes 12292
  10.2 36.4 %copy-start = (s32[1,4]{1,0:T(1,128)S(1)}, s32[1,4]{1,0:T(1,128)}, u32[]{:S(2)}) copy-start(s32[1,4]{1,0:T(1,128)} %plan_ref.3) | copy-start | bytes 52
  16.9 8.2 %collective-permute-start.1 = (bf16[128,1024]{1,0:T(8,128)(2,1)S(1)}, bf16[128,1024]{1,0:T(8,128)(2,1)S(1)}, u32[]{:S(2)}, u32[]{:S(2)}) collective-permute-start(bf16[128,1024]{1,0:T(8,128)(2,1)S(1)} %collective-permute-done.y2_ref), channel_id=1, source_target_pairs={{1,0},{0,1},{3,2},{2,3},{5,4},{4,5},{7,6},{6,7},{9,8},{8,9},{11,10... | collective-permute-start | bytes 786440 | tf_op jit(solution)/shard_map/ppermute | solution.py:240
  25.1 29.5 %collective-permute-start.3 = (bf16[2,128,1024]{2,1,0:T(8,128)(2,1)S(1)}, bf16[2,128,1024]{2,1,0:T(8,128)(2,1)S(1)}, u32[]{:S(2)}, u32[]{:S(2)}) collective-permute-start(bf16[2,128,1024]{2,1,0:T(8,128)(2,1)S(1)} %pad_maximum_fusion), channel_id=1, source_target_pairs={{2,0},{3,1},{4,2},{5,3},{6,4},{7,5},{8,6},{9,7},{10,8},{11,9},{12,... | collective-permute-start | bytes 1572872 | tf_op jit(solution)/shard_map/ppermute | solution.py:240
  29.4 14.4 %collective-permute-start.4 = (bf16[128,1024]{1,0:T(8,128)(2,1)S(1)}, bf16[128,1024]{1,0:T(8,128)(2,1)S(1)}, u32[]{:S(2)}, u32[]{:S(2)}) collective-permute-start(bf16[128,1024]{1,0:T(8,128)(2,1)S(1)} %normalize.1.x_ref), channel_id=1, source_target_pairs={{2,0},{3,1},{4,2},{5,3},{6,4},{7,5},{8,6},{9,7},{10,8},{11,9},{12,... | collective-permute-start | bytes 786440 | tf_op jit(solution)/shard_map/ppermute | solution.py:240
  31.4 15.3 %collective-permute-start.5 = (bf16[128,1024]{1,0:T(8,128)(2,1)S(1)}, bf16[128,1024]{1,0:T(8,128)(2,1)S(1)}, u32[]{:S(2)}, u32[]{:S(2)}) collective-permute-start(bf16[128,1024]{1,0:T(8,128)(2,1)S(1)} %collective-permute-done.y2_ref), channel_id=1, source_target_pairs={{2,0},{3,1},{4,2},{5,3},{6,4},{7,5},{8,6},{9,7},{10,8},{11,9},{12,... | collective-permute-start | bytes 786440 | tf_op jit(solution)/shard_map/ppermute | solution.py:240
